TPU v7x, 256 devices: a whole 4x4x8 slice. The times are simulated.
256 devices in a mesh: ctx: 32 (over y, x, core), head: 4 (over z_lo), dp: 2 (over z_hi).
Axes of the slice: x: 4, y: 4, z: 8 (z_hi: 2, z_lo: 4; z = z_hi * 4 + z_lo), core: 2. Of those that a mesh axis runs over, the one named last changes fastest.
Arguments:
- queries: bfloat16 [2, 8192, 4096], P('dp', 'ctx', 'head'), may hold values from -6 to 6
- keys: bfloat16 [2, 8192, 4096], P('dp', 'ctx', 'head'), may hold values from -6 to 6
- values: bfloat16 [2, 8192, 4096], P('dp', 'ctx', 'head'), may hold values from -6 to 6
- log_decay: float32 [2, 32, 8192], P('dp', 'head', 'ctx'), may hold values from -1.5 to 0
- w_out: bfloat16 [128, 32, 3072], P(('ctx', 'dp'), 'head'), may hold values from -0.09375 to 0.09375
- grad_out: bfloat16 [2, 8192, 3072], P('dp', 'ctx'), may hold values from -6 to 6
Outputs:
- mixed: bfloat16 [2, 8192, 3072], P('dp', 'ctx', 'head')
- query_grad: bfloat16 [2, 8192, 4096], P('dp', 'ctx', 'head')
- key_grad: bfloat16 [2, 8192, 4096], P('dp', 'ctx', 'head')
- value_grad: bfloat16 [2, 8192, 4096], P('dp', 'ctx', 'head')
- w_grad: float32 [128, 32, 3072], P(('ctx', 'dp'), 'head')
All inputs are finite; a program needn't handle non-finite values.
Results may differ from a plain program's by a relative error of at most 0.015.
Values may be sent and summed in bfloat16 or wider, within the bound.
A program may use at most 128 MiB of HBM per device.

v0:
```python
import jax
import jax.numpy as jnp
from jax import lax
from jax.sharding import PartitionSpec as P

DH = 128
BLOCK = 256


def entering_2(array, axis, combine, identity, reverse):
    devices, mine = (lax.axis_size(axis), lax.axis_index(axis))
    everything = jax.tree.map(lambda part: lax.all_gather(part, axis), array)
    start = jax.tree.map(
        lambda part, zero: jnp.broadcast_to(jnp.asarray(zero, part.dtype), part.shape),
        array,
        identity,
    )

    def lap(k, before):
        at = devices - 1 - k if reverse else k
        reached = at > mine if reverse else at < mine
        new = combine(before, jax.tree.map(lambda part: part[at], everything))
        return jax.tree.map(lambda a, b: jnp.where(reached, a, b), new, before)

    return lax.fori_loop(0, devices, lap, start)


def block_weights(cumul):
    width = cumul.shape[-1]
    places = jnp.arange(width)
    lower = places[:, None] >= places[None, :]
    spread = cumul[..., :, None] - cumul[..., None, :]
    return jnp.exp(jnp.where(lower, spread, -jnp.inf))


def forward_join(earlier, later):
    return (earlier[0] * later[0], later[0][:, None, None] * earlier[1] + later[1])


def backward_combine(earlier, later):
    return (earlier[0] * later[0], later[1] + later[0][:, None, None] * earlier[1])


def shards(queries, keys, values, log_decay, w_out, grad_out):
    groups = log_decay.shape[1]
    length_here = queries.shape[1]
    tile_number = length_here // BLOCK
    scale = 1.0 / DH
    query_blocks = queries[0].reshape(tile_number, BLOCK, groups, DH)
    key_blocks = keys[0].reshape(tile_number, BLOCK, groups, DH)
    value_blocks = values[0].reshape(tile_number, BLOCK, groups, DH)
    places = jnp.arange(BLOCK)
    upper = (places[:, None] <= places[None, :]).astype(jnp.float32)
    cumul = jnp.einsum(
        "hnj,jt->hnt",
        log_decay[0].reshape(groups, tile_number, BLOCK),
        upper,
        precision=lax.Precision.HIGHEST,
    )
    weights = block_weights(cumul)
    decay_multiplier = jnp.transpose(scale * jnp.exp(cumul), (1, 2, 0))[..., None]
    tail = jnp.transpose(jnp.exp(cumul[..., -1:] - cumul), (1, 2, 0))[..., None]
    block_decay = jnp.exp(cumul[..., -1])
    ones_decay = jnp.ones((groups,), jnp.float32)
    zero_state = jnp.zeros((groups, DH, DH), jnp.float32)
    scores = jnp.einsum(
        "nthd,njhd->hntj", query_blocks, key_blocks, preferred_element_type=jnp.float32
    )
    probs = (scores * scale * weights).astype(jnp.bfloat16)
    intra = jnp.einsum("hntj,njhd->nthd", probs, value_blocks, preferred_element_type=jnp.float32)
    keys_weighted = (key_blocks * tail).astype(jnp.bfloat16)
    contrib = jnp.einsum(
        "nthd,nthe->hnde", keys_weighted, value_blocks, preferred_element_type=jnp.float32
    )
    total_decay = ones_decay
    total_state = zero_state
    index = 0
    total_state = block_decay[:, index][:, None, None] * total_state + contrib[:, index]
    total_decay = total_decay * block_decay[:, index]
    incoming = entering_2(
        (total_decay, total_state), "ctx", forward_join, (ones_decay, zero_state), False
    )[1]
    running = incoming
    index = 0
    entering = [running]
    state_low = jnp.stack(entering, axis=1).astype(jnp.bfloat16)
    inter = jnp.einsum(
        "nthd,hnde->nthe", query_blocks, state_low, preferred_element_type=jnp.float32
    )
    attended = (intra + inter * decay_multiplier).astype(jnp.bfloat16)
    attended_row_list = attended.reshape(length_here, groups, DH)
    panel = lax.all_gather(w_out, ("ctx", "dp"), axis=0, tiled=True)
    partial_out = jnp.einsum(
        "thd,dho->to", attended_row_list, panel, preferred_element_type=jnp.float32
    )
    mixed = lax.psum_scatter(
        partial_out.astype(jnp.bfloat16), "head", scatter_dimension=1, tiled=True
    )
    cotangent = grad_out[0]
    grad_heads = jnp.einsum(
        "to,dho->thd", cotangent, panel, preferred_element_type=jnp.float32
    ).astype(jnp.bfloat16)
    grad_blocks = grad_heads.reshape(tile_number, BLOCK, groups, DH)
    w_grad = lax.psum_scatter(
        jnp.einsum("thd,to->dho", attended_row_list, cotangent, preferred_element_type=jnp.float32),
        ("ctx", "dp"),
        scatter_dimension=0,
        tiled=True,
    )
    logit_gradient = jnp.einsum(
        "nthe,njhe->hntj", grad_blocks, value_blocks, preferred_element_type=jnp.float32
    )
    dprobs = (logit_gradient * scale * weights).astype(jnp.bfloat16)
    queries_weighted = (query_blocks * decay_multiplier).astype(jnp.bfloat16)
    local_grad = jnp.einsum(
        "nthd,nthe->hnde", queries_weighted, grad_blocks, preferred_element_type=jnp.float32
    )
    faded_carry = ones_decay
    after_state = zero_state
    for index in reversed(range(tile_number)):
        after_state = block_decay[:, index][:, None, None] * after_state + local_grad[:, index]
        faded_carry = faded_carry * block_decay[:, index]
    leaving = entering_2(
        (faded_carry, after_state), "ctx", backward_combine, (ones_decay, zero_state), True
    )[1]
    exiting = []
    running = leaving
    for index in reversed(range(tile_number)):
        exiting = [running] + exiting
        running = block_decay[:, index][:, None, None] * running + local_grad[:, index]
    back_low = jnp.stack(exiting, axis=1).astype(jnp.bfloat16)
    query_grad = (
        jnp.einsum("hntj,njhd->nthd", dprobs, key_blocks, preferred_element_type=jnp.float32)
        + jnp.einsum("nthe,hnde->nthd", grad_blocks, state_low, preferred_element_type=jnp.float32)
        * decay_multiplier
    )
    key_grad = jnp.einsum(
        "hntj,nthd->njhd", dprobs, query_blocks, preferred_element_type=jnp.float32
    ) + tail * jnp.einsum(
        "nthe,hnde->nthd", value_blocks, back_low, preferred_element_type=jnp.float32
    )
    value_grad = jnp.einsum(
        "hntj,nthe->njhe", probs, grad_blocks, preferred_element_type=jnp.float32
    ) + tail * jnp.einsum(
        "nthd,hnde->nthe", key_blocks, back_low, preferred_element_type=jnp.float32
    )
    flat = (1, length_here, groups * DH)
    return (
        mixed[None],
        query_grad.astype(jnp.bfloat16).reshape(flat),
        key_grad.astype(jnp.bfloat16).reshape(flat),
        value_grad.astype(jnp.bfloat16).reshape(flat),
        w_grad,
    )


def solution(mesh):
    return jax.shard_map(
        shards,
        mesh=mesh,
        in_specs=(
            P("dp", "ctx", "head"),
            P("dp", "ctx", "head"),
            P("dp", "ctx", "head"),
            P("dp", "head", "ctx"),
            P(("ctx", "dp"), "head", None),
            P("dp", "ctx", None),
        ),
        out_specs=(
            P("dp", "ctx", "head"),
            P("dp", "ctx", "head"),
            P("dp", "ctx", "head"),
            P("dp", "ctx", "head"),
            P(("ctx", "dp"), "head", None),
        ),
        check_vma=False,
    )
```

profile of v0, /device:TPU:1, one launch (start us, length us, event | category | flops | bytes accessed | tf_op | source)
XLA Modules:
  0.0 551.8 jit_solution(11020169705880743914)
XLA Ops:
  9.1 1.3 copy.96
  12.5 1.2 copy.94
  13.7 104.7 %all-gather.7.cloned.1.call-done = bf16[128,8,3072]{2,1,0:T(8,128)(2,1)} async-done(((bf16[2,8,3072]{2,1,0:T(8,128)(2,1)}), bf16[128,8,3072]{2,1,0:T(8,128)(2,1)}) %all-gather.7.cloned.1.call-update) | async-done | bytes 6291472 | tf_op jit(solution)/shard_map/all_gather | solution.py:92
  118.4 4.6 fusion.11
  126.6 63.6 %all-reduce = f32[256]{0:T(256)S(1)} all-reduce(f32[256]{0:T(256)S(1)} %dynamic-update-slice), channel_id=2, replica_groups=mesh['ctx'=32,'head'=4,'dp'=2] {'ctx'}, use_global_device_ids=true, to_apply=%add | all-reduce | flops 256 | bytes 2048
  190.3 1.8 multiply_convert_fusion.1
  193.1 1.4 convolution_bitcast_fusion.8
  194.5 39.3 %while.30 = (s32[]{:T(128)}, f32[8,128,128]{2,1,0:T(8,128)S(1)}, s32[]{:T(128)}, f32[32,8]{1,0:T(8,128)S(1)}, f32[32,8,128,128]{3,2,1,0:T(8,128)}, /*index=5*/s32[]{:T(128)}, s32[]{:T(128)}) while((s32[]{:T(128)}, f32[8,128,128]{2,1,0:T(8,128)S(1)}, s32[]{:T(128)}, f32[32,8]{1,0:T(8,128)S(1)}, f32[32,8,128,128]{3,2,1,0:T(8,128)}, ...), condition=%wide.region_1.2_spmd.clone, body=%wide.region_0.1_spmd.clone.sunk | while | flops 524292 | bytes 1573073 | solution.py:25
  196.9 1.2 fusion.58
  198.2 1.2 fusion.58
  200.6 1.2 fusion.58
  203.0 1.2 fusion.58
  205.5 1.2 fusion.58
  206.7 1.2 fusion.58
  208.0 1.3 fusion.58
  211.7 1.2 fusion.58
  212.9 1.2 fusion.58
  214.2 1.2 fusion.58
  216.6 1.2 fusion.58
  217.9 1.2 fusion.58
  219.1 1.2 fusion.58
  232.5 1.3 fusion.58
  233.8 1.9 fusion.25
  236.5 17.9 %fusion.7 = bf16[256,3072]{1,0:T(8,128)(2,1)} fusion(bf16[256,8,128]{2,0,1:T(8,128)(2,1)S(1)} %fusion.25, bf16[128,8,3072]{2,1,0:T(8,128)(2,1)} %all-gather.7.cloned.1.call-done), kind=kOutput, calls=%fused_computation.10 | convolution fusion | flops 1611399168 | bytes 8388608 | tf_op jit(solution)/shard_map/thd,dho->to/dot_general | solution.py:93
  255.5 6.4 %convolution_bitcast_fusion = f32[128,8,3072]{2,0,1:T(8,128)} fusion(bf16[256,8,128]{2,0,1:T(8,128)(2,1)S(1)} %copy-done.10, bf16[1,256,3072]{2,1,0:T(8,128)(2,1)S(1)} %copy-done), kind=kOutput, calls=%fused_computation.6 | convolution fusion | flops 1610612736 | bytes 14680064 | tf_op jit(solution)/shard_map/thd,to->dho/dot_general | solution.py:105
  261.9 16.7 %copy.81 = f32[128,8,3072]{2,1,0:T(8,128)} copy(f32[128,8,3072]{2,0,1:T(8,128)} %convolution_bitcast_fusion) | data formatting | bytes 25165824 | tf_op jit(solution)/shard_map/thd,to->dho/transpose | solution.py:105
  280.7 1.3 convolution_bitcast_fusion.5
  282.4 1.3 convolution_bitcast_fusion.6
  285.9 39.4 %while.31 = (s32[]{:T(128)}, f32[8,128,128]{2,1,0:T(8,128)S(1)}, s32[]{:T(128)}, f32[32,8,128,128]{3,2,1,0:T(8,128)}, f32[32,8]{1,0:T(8,128)S(1)}, /*index=5*/s32[]{:T(128)}, s32[]{:T(128)}, s32[]{:T(128)}, s32[]{:T(128)}) while((s32[]{:T(128)}, f32[8,128,128]{2,1,0:T(8,128)S(1)}, s32[]{:T(128)}, f32[32,8,128,128]{3,2,1,0:T(8,128)}, ...), condition=%wide.region_4.5_spmd.clone, body=%wide.region_3.4_spmd.clone.sunk | while | flops 524296 | bytes 1573135 | solution.py:25
  285.9 1.3 fusion.59
  287.2 1.2 fusion.59
  288.5 1.2 fusion.59
  289.7 1.2 fusion.59
  290.9 1.2 fusion.59
  292.1 1.2 fusion.59
  293.4 1.2 fusion.59
  294.6 1.2 fusion.59
  295.8 1.2 fusion.59
  297.0 1.2 fusion.59
  298.3 1.2 fusion.59
  299.5 1.2 fusion.59
  300.7 1.2 fusion.59
  302.0 1.2 fusion.59
  303.2 1.2 fusion.59
  304.4 1.2 fusion.59
  305.7 1.2 fusion.59
  306.9 1.2 fusion.59
  308.1 1.2 fusion.59
  309.3 1.2 fusion.59
  310.6 1.2 fusion.59
  311.8 1.2 fusion.59
  313.0 1.2 fusion.59
  314.3 1.2 fusion.59
  315.5 1.2 fusion.59
  316.7 1.2 fusion.59
  317.9 1.2 fusion.59
  319.2 1.2 fusion.59
  320.4 1.2 fusion.59
  321.6 1.2 fusion.59
  322.8 1.2 fusion.59
  324.1 1.2 fusion.59
  326.4 2.2 copy.83
  328.6 1.6 fusion.22
  331.2 214.1 %reduce-scatter.5.cloned.1.call-done = f32[2,8,3072]{2,1,0:T(8,128)} async-done(((f32[128,8,3072]{2,1,0:T(8,128)}), f32[2,8,3072]{2,1,0:T(8,128)}) %reduce-scatter.5.cloned.1.call-update) | async-done | bytes 196624 | tf_op jit(solution)/shard_map/reduce_scatter | solution.py:104
  (152 shorter events, 38.1 us)
Async XLA Ops:
  7.2 111.3 %copy-start = (bf16[1,256,3072]{2,1,0:T(8,128)(2,1)S(1)}, bf16[1,256,3072]{2,1,0:T(8,128)(2,1)}, u32[]{:S(2)}) copy-start(bf16[1,256,3072]{2,1,0:T(8,128)(2,1)} %param.15) | copy-start | bytes 4718596
  7.2 3.6 copy-start.16
  7.2 111.2 %all-gather.7.cloned.1.call-start = ((), (), s32[]{:S(2)}) async-start(), calls=%async_computation.2 | async-start | bytes 6389760 | tf_op jit(solution)/shard_map/all_gather | solution.py:92
  7.9 186.6 %all-gather.9.cloned.1.call-start = ((), (), s32[]{:S(2)}) async-start(), calls=%async_computation.5 | async-start | bytes 17301504 | tf_op jit(solution)/shard_map/all_gather | solution.py:12
  9.1 3.3 copy-start.4
  10.8 1.6 copy-start.14
  12.4 273.4 %all-gather.11.cloned.1.call-start = ((), (), s32[]{:S(2)}) async-start(), calls=%async_computation.6 | async-start | bytes 17301504 | tf_op jit(solution)/shard_map/all_gather | solution.py:12
  13.7 220.1 %copy-start.2 = (bf16[1,256,1024]{1,2,0:T(8,128)(2,1)}, bf16[1,256,1024]{1,2,0:T(8,128)(2,1)S(1)}, u32[]{:S(2)}) copy-start(bf16[1,256,1024]{1,2,0:T(8,128)(2,1)S(1)} %copy.94) | copy-start | bytes 1572868
  123.0 0.8 copy-start.11
  123.0 2.0 copy-start.17
  125.0 206.2 %reduce-scatter.3.cloned.1.call-start = ((), (), s32[]{:S(2)}) async-start(), calls=%async_computation.3 | async-start | bytes 1966080 | tf_op jit(solution)/shard_map/reduce_scatter | solution.py:96
  192.1 1.0 copy-start.6
  235.7 0.8 copy-start.9
  254.4 1.1 copy-start.10
  254.5 290.8 %reduce-scatter.5.cloned.1.call-start = ((), (), s32[]{:S(2)}) async-start(), calls=%async_computation.4 | async-start | bytes 12779520 | tf_op jit(solution)/shard_map/reduce_scatter | solution.py:104
  278.6 1.0 copy-start.12
  279.6 1.0 copy-start.3
  280.7 1.3 copy-start.7
  280.7 1.7 copy-start.13
  280.7 3.0 copy-start.15
  285.9 39.4 %copy-start.8 = (f32[1,256,8,128]{1,3,2,0:T(8,128)S(1)}, f32[1,256,8,128]{1,3,2,0:T(8,128)}, u32[]{:S(2)}) copy-start(f32[1,256,8,128]{1,3,2,0:T(8,128)} %convolution_bitcast_fusion.5) | copy-start | bytes 3145732
  325.3 3.3 copy-start.5
  326.4 218.8 %copy-start.1 = (bf16[1,256,3072]{2,1,0:T(8,128)(2,1)S(1)}, bf16[1,256,3072]{2,1,0:T(8,128)(2,1)}, u32[]{:S(2)}) copy-start(bf16[1,256,3072]{2,1,0:T(8,128)(2,1)} %param.15) | copy-start | bytes 4718596
Sparse Core Ops, SparseCore 0:
  11.8 106.5 all-gather.6
  121.5 71.6 all-gather.8
  195.8 76.6 all-gather.10
  275.5 39.5 reduce-scatter.2
  321.7 223.4 reduce-scatter.4
where the time goes:
time: 555 us; the launch traced here: 552 us
  waiting for transfers between devices  320 us (58%)
  other arithmetic  76 us (14%)
  blocking collectives  63.6 us (11%)
  matrix products  43.5 us (8%)
  local copies, waits for them, and re-layouts  31.6 us (6%)
  between operations  14.7 us (3%)
    reduce_scatter x1, waiting for transfers between devices, shards(): lax.psum_scatter(jnp.einsum('thd,to->dho', attended_row_list, cotangent,...  214 us
    all_gather x1, waiting for transfers between devices, shards(): panel = lax.all_gather(w_out, ('ctx', 'dp'), axis=0, tiled=True)  105 us
    select_n x64, other arithmetic, lap(): return jax.tree.map(lambda a, b: jnp.where(reached, a, b), new, before)  75.7 us
    unnamed x1, blocking collectives  63.6 us
    dot_general x1, matrix products, shards(): jnp.einsum('thd,dho->to', attended_row_list, panel, preferred_element_typ...  17.9 us
    transpose x1, local copies, waits for them, and re-layouts, shards(): jnp.einsum('thd,to->dho', attended_row_list, cotangent, preferred_element...  16.7 us
    unnamed x44, local copies, waits for them, and re-layouts  12.5 us
  transfers between devices with their start and end apart: 5, of which 2 were waited for; matrix products, arithmetic and copies ran while one was open for 26% of the time, Pallas kernels for 0%

commit v1 on v0

--- a/solution.py
+++ b/solution.py
@@ -89,7 +89,10 @@
     )
     attended = (intra + inter * decay_multiplier).astype(jnp.bfloat16)
     attended_row_list = attended.reshape(length_here, groups, DH)
-    panel = lax.all_gather(w_out, ("ctx", "dp"), axis=0, tiled=True)
+    peers = lax.axis_size(("ctx", "dp"))
+    tiles = jnp.stack([w_out for _ in range(peers)])
+    tiles = lax.all_to_all(tiles, ("ctx", "dp"), split_axis=0, concat_axis=0)
+    panel = jnp.concatenate(tiles, axis=0)
     partial_out = jnp.einsum(
         "thd,dho->to", attended_row_list, panel, preferred_element_type=jnp.float32
     )

time: 555 us -> 596 us (1.074)
  local copies, waits for them, and re-layouts: 31.6 us -> 53.7 us
  blocking collectives: 63.6 us -> 83.2 us
  starting transfers between devices: 0.42 us -> 16.1 us
  matrix products: 43.5 us -> 33 us
  waiting for transfers between devices: 320 us -> 313 us
    all_to_all x0 -> x1, waiting for transfers between devices: none -> 120 us  [shards(): tiles = lax.all_to_all(tiles, ('ctx', 'dp'), split_axis=0, concat_axis=0)]
    all_gather x1 -> x0, waiting for transfers between devices: 105 us -> none  [shards(): panel = lax.all_gather(w_out, ('ctx', 'dp'), axis=0, tiled=True)]
    reduce_scatter x1, waiting for transfers between devices: 214 us -> 193 us  [shards(): lax.psum_scatter(jnp.einsum('thd,to->dho', attended_row_list, cotangent,...]
    unnamed x1, blocking collectives: 63.6 us -> 83.2 us
    all_to_all x0 -> x1, starting transfers between devices: none -> 15.8 us  [shards(): tiles = lax.all_to_all(tiles, ('ctx', 'dp'), split_axis=0, concat_axis=0)]
    reshape x1 -> x2, local copies, waits for them, and re-layouts: 1.25 us -> 14.9 us  [the longest x1 13.6 us: shards(): panel = jnp.concatenate(tiles, axis=0)]
    dot_general x1, matrix products: 17.9 us -> 5.71 us  [shards(): jnp.einsum('thd,dho->to', attended_row_list, panel, preferred_element_typ...]
    all_to_all x0 -> x1, local copies, waits for them, and re-layouts: none -> 6.91 us  [shards(): tiles = lax.all_to_all(tiles, ('ctx', 'dp'), split_axis=0, concat_axis=0)]
where the time goes in v1:
time: 596 us; the launch traced here: 592 us
  waiting for transfers between devices  313 us (53%)
  blocking collectives  83.2 us (14%)
  other arithmetic  76.1 us (13%)
  local copies, waits for them, and re-layouts  53.7 us (9%)
  matrix products  33 us (6%)
  starting transfers between devices  16.1 us (3%)
  between operations  14.7 us (2%)
    reduce_scatter x1, waiting for transfers between devices, shards(): lax.psum_scatter(jnp.einsum('thd,to->dho', attended_row_list, cotangent,...  193 us
    all_to_all x1, waiting for transfers between devices, shards(): tiles = lax.all_to_all(tiles, ('ctx', 'dp'), split_axis=0, concat_axis=0)  120 us
    unnamed x1, blocking collectives  83.2 us
    select_n x64, other arithmetic, lap(): return jax.tree.map(lambda a, b: jnp.where(reached, a, b), new, before)  75.7 us
    transpose x1, local copies, waits for them, and re-layouts, shards(): jnp.einsum('thd,to->dho', attended_row_list, cotangent, preferred_element...  16.7 us
    all_to_all x1, starting transfers between devices, shards(): tiles = lax.all_to_all(tiles, ('ctx', 'dp'), split_axis=0, concat_axis=0)  15.8 us
    reshape x1, local copies, waits for them, and re-layouts, shards(): panel = jnp.concatenate(tiles, axis=0)  13.6 us
  transfers between devices with their start and end apart: 5, of which 2 were waited for; matrix products, arithmetic and copies ran while one was open for 26% of the time, Pallas kernels for 0%

profile of v1, /device:TPU:1, one launch (start us, length us, event | category | flops | bytes accessed | tf_op | source)
XLA Modules:
  0.0 591.9 jit_solution(16406023710529506311)
XLA Ops:
  10.0 1.3 copy.94
  12.6 4.4 stack.2
  17.0 15.8 %all-to-all-start = ((bf16[64,2,8,3072]{3,1,2,0:T(2,128)(2,1)}), bf16[64,2,8,3072]{3,1,2,0:T(2,128)(2,1)}, u32[]{:S(2)}, u32[]{:S(2)}) async-start(bf16[64,2,8,3072]{3,1,2,0:T(2,128)(2,1)} %stack.2), calls=%async_computation | async-start | bytes 12582912 | tf_op jit(solution)/shard_map/all_to_all | solution.py:94
  32.8 1.2 copy.92
  34.1 120.0 %all-to-all-done = bf16[64,2,8,3072]{3,1,2,0:T(2,128)(2,1)} async-done(((bf16[64,2,8,3072]{3,1,2,0:T(2,128)(2,1)}), bf16[64,2,8,3072]{3,1,2,0:T(2,128)(2,1)}, u32[]{:S(2)}, u32[]{:S(2)}) %all-to-all-start) | async-done | bytes 6291488 | tf_op jit(solution)/shard_map/all_to_all | solution.py:94
  154.1 6.9 %copy.68 = bf16[64,2,8,3072]{3,1,0,2:T(2,128)(2,1)} copy(bf16[64,2,8,3072]{3,1,2,0:T(2,128)(2,1)} %all-to-all-done) | data formatting | bytes 12582912 | tf_op jit(solution)/shard_map/all_to_all | solution.py:94
  161.0 13.6 %reshape.169 = bf16[128,8,3072]{2,0,1:T(8,128)(2,1)} reshape(bf16[64,2,8,3072]{3,1,0,2:T(2,128)(2,1)} %copy.68) | data formatting | bytes 12582912 | tf_op jit(solution)/shard_map/reshape | solution.py:95
  174.6 4.6 fusion.18
  182.0 83.2 %all-reduce = f32[256]{0:T(256)S(1)} all-reduce(f32[256]{0:T(256)S(1)} %dynamic-update-slice), channel_id=2, replica_groups=mesh['ctx'=32,'head'=4,'dp'=2] {'ctx'}, use_global_device_ids=true, to_apply=%add | all-reduce | flops 256 | bytes 2048
  265.3 1.8 multiply_convert_fusion.1
  268.1 1.4 convolution_bitcast_fusion.9
  269.5 39.1 %while.30 = (s32[]{:T(128)}, f32[8,128,128]{2,1,0:T(8,128)S(1)}, s32[]{:T(128)}, f32[32,8]{1,0:T(8,128)S(1)}, f32[32,8,128,128]{3,2,1,0:T(8,128)}, /*index=5*/s32[]{:T(128)}, s32[]{:T(128)}) while((s32[]{:T(128)}, f32[8,128,128]{2,1,0:T(8,128)S(1)}, s32[]{:T(128)}, f32[32,8]{1,0:T(8,128)S(1)}, f32[32,8,128,128]{3,2,1,0:T(8,128)}, ...), condition=%wide.region_1.2_spmd.clone, body=%wide.region_0.1_spmd.clone.sunk | while | flops 524292 | bytes 1573073 | solution.py:25
  270.7 1.2 fusion.55
  271.9 1.2 fusion.55
  273.2 1.3 fusion.55
  274.5 1.2 fusion.55
  275.8 1.2 fusion.55
  277.0 1.2 fusion.55
  278.2 1.2 fusion.55
  279.4 1.2 fusion.55
  280.6 1.2 fusion.55
  281.8 1.2 fusion.55
  283.1 1.2 fusion.55
  284.3 1.2 fusion.55
  285.5 1.2 fusion.55
  286.7 1.2 fusion.55
  287.9 1.2 fusion.55
  289.1 1.2 fusion.55
  290.4 1.2 fusion.55
  291.6 1.2 fusion.55
  292.8 1.2 fusion.55
  294.0 1.2 fusion.55
  295.2 1.2 fusion.55
  296.5 1.2 fusion.55
  297.7 1.2 fusion.55
  300.1 1.2 fusion.55
  303.8 1.2 fusion.55
  305.0 1.2 fusion.55
  308.6 1.7 fusion.21
  310.3 5.7 fusion.2
  316.3 6.3 %convolution_bitcast_fusion = f32[128,8,3072]{2,0,1:T(8,128)} fusion(bf16[256,8,128]{2,0,1:T(8,128)(2,1)S(1)} %fusion.21, bf16[1,256,3072]{2,1,0:T(8,128)(2,1)S(1)} %copy-done), kind=kOutput, calls=%fused_computation.6 | convolution fusion | flops 1610612736 | bytes 14680064 | tf_op jit(solution)/shard_map/thd,to->dho/dot_general | solution.py:108
  322.6 16.7 %copy.81 = f32[128,8,3072]{2,1,0:T(8,128)} copy(f32[128,8,3072]{2,0,1:T(8,128)} %convolution_bitcast_fusion) | data formatting | bytes 25165824 | tf_op jit(solution)/shard_map/thd,to->dho/transpose | solution.py:108
  340.3 2.5 convolution_bitcast_fusion.7
  343.6 1.4 convolution_bitcast_fusion.6
  347.2 39.5 %while.31 = (s32[]{:T(128)}, f32[8,128,128]{2,1,0:T(8,128)S(1)}, s32[]{:T(128)}, f32[32,8,128,128]{3,2,1,0:T(8,128)}, f32[32,8]{1,0:T(8,128)S(1)}, /*index=5*/s32[]{:T(128)}, s32[]{:T(128)}, s32[]{:T(128)}, s32[]{:T(128)}) while((s32[]{:T(128)}, f32[8,128,128]{2,1,0:T(8,128)S(1)}, s32[]{:T(128)}, f32[32,8,128,128]{3,2,1,0:T(8,128)}, ...), condition=%wide.region_4.5_spmd.clone, body=%wide.region_3.4_spmd.clone.sunk | while | flops 524296 | bytes 1573135 | solution.py:25
  347.2 1.3 fusion.56
  348.5 1.2 fusion.56
  352.2 1.2 fusion.56
  354.7 1.2 fusion.56
  371.8 1.2 fusion.56
  373.1 1.2 fusion.56
  374.3 1.2 fusion.56
  375.5 1.2 fusion.56
  376.8 1.2 fusion.56
  378.0 1.2 fusion.56
  379.3 1.2 fusion.56
  380.5 1.2 fusion.56
  381.8 1.2 fusion.56
  383.0 1.2 fusion.56
  384.2 1.2 fusion.56
  385.5 1.2 fusion.56
  387.9 2.2 copy.84
  390.0 1.6 fusion.16
  392.6 192.8 %reduce-scatter.5.cloned.1.call-done = f32[2,8,3072]{2,1,0:T(8,128)} async-done(((f32[128,8,3072]{2,1,0:T(8,128)}), f32[2,8,3072]{2,1,0:T(8,128)}) %reduce-scatter.5.cloned.1.call-update) | async-done | bytes 196624 | tf_op jit(solution)/shard_map/reduce_scatter | solution.py:107
  (149 shorter events, 40.0 us)
Async XLA Ops:
  7.2 167.5 %copy-start = (bf16[1,256,3072]{2,1,0:T(8,128)(2,1)S(1)}, bf16[1,256,3072]{2,1,0:T(8,128)(2,1)}, u32[]{:S(2)}) copy-start(bf16[1,256,3072]{2,1,0:T(8,128)(2,1)} %param.15) | copy-start | bytes 4718596
  7.2 262.3 %all-gather.6.cloned.1.call-start = ((), (), s32[]{:S(2)}) async-start(), calls=%async_computation.5 | async-start | bytes 17301504 | tf_op jit(solution)/shard_map/all_gather | solution.py:12
  9.7 2.8 copy-start.7
  9.7 2.8 copy-start.13
  10.0 7.0 %copy-start.11 = (bf16[256,8,128]{0,2,1:T(8,128)(2,1)}, bf16[256,8,128]{0,2,1:T(8,128)(2,1)S(1)}, u32[]{:S(2)}) copy-start(bf16[256,8,128]{0,2,1:T(8,128)(2,1)S(1)} %copy.62) | copy-start | bytes 1572868
  11.4 255.8 %copy-start.2 = (bf16[32,8,8,128]{3,2,1,0:T(8,128)(2,1)}, bf16[32,8,8,128]{3,2,1,0:T(8,128)(2,1)S(1)}, u32[]{:S(2)}) copy-start(bf16[32,8,8,128]{3,2,1,0:T(8,128)(2,1)S(1)} %copy.94) | copy-start | bytes 1572868
  17.0 137.1 %all-to-all-start = ((bf16[64,2,8,3072]{3,1,2,0:T(2,128)(2,1)}), bf16[64,2,8,3072]{3,1,2,0:T(2,128)(2,1)}, u32[]{:S(2)}, u32[]{:S(2)}) async-start(bf16[64,2,8,3072]{3,1,2,0:T(2,128)(2,1)} %stack.2), calls=%async_computation | async-start | bytes 12582912 | tf_op jit(solution)/shard_map/all_to_all | solution.py:94
  32.8 314.4 %all-gather.8.cloned.1.call-start = ((), (), s32[]{:S(2)}) async-start(), calls=%async_computation.6 | async-start | bytes 17301504 | tf_op jit(solution)/shard_map/all_gather | solution.py:12
  179.2 1.2 copy-start.5
  179.2 1.2 copy-start.14
  180.4 212.3 %reduce-scatter.3.cloned.1.call-start = ((), (), s32[]{:S(2)}) async-start(), calls=%async_computation.3 | async-start | bytes 1966080 | tf_op jit(solution)/shard_map/reduce_scatter | solution.py:99
  267.1 1.0 copy-start.10
  316.1 269.3 %reduce-scatter.5.cloned.1.call-start = ((), (), s32[]{:S(2)}) async-start(), calls=%async_computation.4 | async-start | bytes 12779520 | tf_op jit(solution)/shard_map/reduce_scatter | solution.py:107
  339.3 1.0 copy-start.6
  339.3 3.5 copy-start.3
  343.6 1.4 copy-start.12
  347.2 39.5 %copy-start.8 = (bf16[32,8,8,128]{3,2,1,0:T(8,128)(2,1)S(1)}, bf16[32,8,8,128]{3,2,1,0:T(8,128)(2,1)}, u32[]{:S(2)}) copy-start(bf16[32,8,8,128]{3,2,1,0:T(8,128)(2,1)} %copy-done.7) | copy-start | bytes 1572868
  347.2 39.5 %copy-start.9 = (f32[1,256,8,128]{1,3,2,0:T(8,128)S(1)}, f32[1,256,8,128]{1,3,2,0:T(8,128)}, u32[]{:S(2)}) copy-start(f32[1,256,8,128]{1,3,2,0:T(8,128)} %convolution_bitcast_fusion.7) | copy-start | bytes 3145732
  386.7 3.4 copy-start.4
  387.9 197.5 %copy-start.1 = (bf16[1,256,3072]{2,1,0:T(8,128)(2,1)S(1)}, bf16[1,256,3072]{2,1,0:T(8,128)(2,1)}, u32[]{:S(2)}) copy-start(bf16[1,256,3072]{2,1,0:T(8,128)(2,1)} %param.15) | copy-start | bytes 4718596
Sparse Core Ops, SparseCore 0:
  12.6 146.2 all-gather.5
  180.5 97.6 all-gather.7
  316.2 38.9 reduce-scatter.2
  361.9 223.4 reduce-scatter.4
